TPU v7x, 32 devices: a whole 2x2x4 slice. The times are simulated.
32 devices in a mesh: dp: 8 (over y, x, core), ctx: 4 (over z).
Axes of the slice: x: 2, y: 2, z: 4, core: 2. Of those that a mesh axis runs over, the one named last changes fastest.
Arguments:
- inputs: bfloat16 [8, 512, 2048], P('dp', 'ctx'), may hold values from -6 to 6
- segment: int32 [8, 512], P('dp', 'ctx'), may hold values from 0 to 3, as said below
- w_qkv: bfloat16 [2048, 6144], P(('dp', 'ctx')), may hold values from -0.125 to 0.125
- w_out: bfloat16 [2048, 2048], P(('dp', 'ctx')), may hold values from -0.125 to 0.125
- w_gate: bfloat16 [2048, 8192], P('dp', 'ctx'), may hold values from -0.125 to 0.125
- w_up: bfloat16 [2048, 8192], P('dp', 'ctx'), may hold values from -0.125 to 0.125
- w_down_t: bfloat16 [2048, 8192], P('dp', 'ctx'), may hold values from -0.0625 to 0.0625
- gains: float32 [4, 2048], replicated, may hold values from 0.25 to 1.75
- cotangent: bfloat16 [8, 512, 2048], P('dp', 'ctx'), may hold values from -6 to 6
Outputs:
- output: bfloat16 [8, 512, 2048], P('dp', 'ctx')
- input_grad: float32 [8, 512, 2048], P('dp', 'ctx')
- grad_qkv: float32 [2048, 6144], P(('dp', 'ctx'))
- grad_out: float32 [2048, 2048], P(('dp', 'ctx'))
- grad_gate: float32 [2048, 8192], P('dp', 'ctx')
- grad_up: float32 [2048, 8192], P('dp', 'ctx')
- grad_down_t: float32 [2048, 8192], P('dp', 'ctx')
- grad_gains: float32 [4, 2048], replicated
Inputs may be any that keep to these rules, and one draw needn't show every extreme that they name: `segment`: in every sequence ids 1, 2 and 3 mark three documents in this order, each of one position or more, and 0 marks padding, one position or more at the sequence's end.
All inputs are finite; a program needn't handle non-finite values.
Results may differ from a plain program's by a relative error of at most 0.015.
Values may be sent and summed in bfloat16 or wider, within the bound.
A program may use at most 704 MiB of HBM per device.

v0:
```python
import jax
import jax.numpy as jnp
from jax import lax
from jax.sharding import Mesh
from jax.sharding import PartitionSpec as P

HEAD_DIM = 128
EPS = 1e-06
ROPE_BASE = 500000.0
F32 = jnp.float32
BF16 = jnp.bfloat16
GROUP = ("core", "ctx")
ALL = ("chip", "core", "ctx")


def rope_tables(positions):
    half = HEAD_DIM // 2
    frequency = ROPE_BASE ** (-(jnp.arange(half, dtype=F32) * 2.0 / HEAD_DIM))
    angles = positions[:, None] * frequency[None, :]
    cosine = jnp.cos(angles)
    sine = jnp.sin(angles)
    return (jnp.concatenate([cosine, cosine], 1), jnp.concatenate([sine, sine], 1))


def rotate(values, cosine, sine):
    half = HEAD_DIM // 2
    turned = jnp.concatenate([-values[..., half:], values[..., :half]], -1)
    return values * cosine + turned * sine


def rotate_back(values, cosine, sine):
    half = HEAD_DIM // 2
    scaled = values * sine
    turned = jnp.concatenate([scaled[..., half:], -scaled[..., :half]], -1)
    return values * cosine + turned


def dot(left, right):
    return jnp.dot(left, right, preferred_element_type=F32)


def dot_rows(left, right):
    return lax.dot_general(left, right, (((1,), (1,)), ((), ())), preferred_element_type=F32)


def dot_first(left, right):
    return lax.dot_general(left, right, (((0,), (0,)), ((), ())), preferred_element_type=F32)


def gather(values, axes):
    return lax.all_gather(values, axes, axis=0, tiled=True)


def scatter_sum(values, axes):
    return lax.psum_scatter(values, axes, scatter_dimension=0, tiled=True)


def norm_factor(values):
    return lax.rsqrt(jnp.mean(values * values, axis=-1, keepdims=True) + EPS)


def norm_back(values, factor, gain, grad):
    normed = values * factor
    scaled = gain * grad
    back = factor * (scaled - normed * jnp.mean(scaled * normed, axis=-1, keepdims=True))
    return (back, jnp.sum(grad * normed, axis=0))


def per_device(inputs, segment, w_qkv, w_out, w_gate, w_up, w_down_t, gains, cotangent):
    rows, width = inputs.shape[1:]
    cores = lax.axis_size("core")
    spans = lax.axis_size("ctx")
    members = cores * spans
    length = rows * spans
    total_rows = cores * length
    part = width // members
    heads = part // HEAD_DIM
    member = lax.axis_index(GROUP)
    tokens = inputs[0]
    qkv_rows = w_qkv.shape[0]
    qkv_cut = w_qkv.reshape(qkv_rows, 3, members, part).transpose(2, 0, 1, 3)
    qkv_cut = qkv_cut.reshape(members, qkv_rows, 3 * part)
    qkv_cut = lax.all_to_all(qkv_cut, GROUP, 0, 0, tiled=True)
    qkv_w = gather(qkv_cut.reshape(members * qkv_rows, 3 * part), "chip")
    tokens_all = gather(tokens, GROUP)
    out_full = gather(w_out, ALL)
    out_w = lax.dynamic_slice_in_dim(out_full, member * part, part, 0)
    hidden = w_gate.shape[1] // cores
    gate_up = jnp.concatenate(
        [w_gate.reshape(-1, cores, 1, hidden), w_up.reshape(-1, cores, 1, hidden)], 2
    ).reshape(-1, cores * 2 * hidden)
    gate_up = lax.all_to_all(gate_up, "core", 1, 0, tiled=True)
    gate_up_w = gather(gate_up, "chip")
    down_w = gather(lax.all_to_all(w_down_t, "core", 1, 0, tiled=True), "chip")
    mixed = dot(tokens_all, qkv_w)
    query_raw = mixed[:, :part]
    key_raw = mixed[:, part : 2 * part]
    value_low = mixed[:, 2 * part :].astype(BF16)
    squares = jnp.stack([jnp.sum(query_raw * query_raw, 1), jnp.sum(key_raw * key_raw, 1)])
    squares = lax.psum(squares, GROUP)
    factors = lax.rsqrt(squares / width + EPS)
    gain_q = lax.dynamic_slice_in_dim(gains[0], member * part, part)
    gain_k = lax.dynamic_slice_in_dim(gains[1], member * part, part)
    places = jnp.arange(length, dtype=jnp.int32)
    cosine, sine = rope_tables(places.astype(F32))
    cosine, sine = (cosine[None, :, None, :], sine[None, :, None, :])
    shape = (cores, length, heads, HEAD_DIM)
    query_factor, key_factor = (factors[0][:, None], factors[1][:, None])
    query_low = rotate((query_raw * query_factor * gain_q).reshape(shape), cosine, sine).astype(
        BF16
    )
    key_low = rotate((key_raw * key_factor * gain_k).reshape(shape), cosine, sine).astype(BF16)
    value_low = value_low.reshape(shape)
    ids = gather(segment[0], GROUP).reshape(cores, length)
    allowed = (
        (ids[:, :, None] == ids[:, None, :])
        & (places[None, None, :] <= places[None, :, None])
        & ((ids[:, None, :] != 0) | (places[None, None, :] == places[None, :, None]))
    )[:, None]
    scale = HEAD_DIM ** (-0.5)
    scores = jnp.einsum("bqhd,bkhd->bhqk", query_low, key_low, preferred_element_type=F32) * scale
    masked = jnp.where(allowed, scores, -1e30)
    row_max = jnp.max(masked, axis=-1, keepdims=True)
    weights = jnp.where(allowed, jnp.exp(masked - row_max), 0.0)
    shares = weights / jnp.sum(weights, axis=-1, keepdims=True)
    shares_low = shares.astype(BF16)
    attended = jnp.einsum("bhqk,bkhd->bqhd", shares_low, value_low, preferred_element_type=F32)
    attended_low = attended.reshape(total_rows, part).astype(BF16)
    projected = scatter_sum(dot(attended_low, out_w).astype(BF16), GROUP).astype(F32)
    tokens_wide = tokens.astype(F32)
    proj_factor = norm_factor(projected)
    residual = tokens_wide + projected * proj_factor * gains[2]
    residual_all = gather(residual.astype(BF16), GROUP)
    gate_up_out = dot(residual_all, gate_up_w)
    gate, up_part = (gate_up_out[:, :hidden], gate_up_out[:, hidden:])
    sigmoid = 1.0 / (1.0 + jnp.exp(-gate))
    activated = (gate * sigmoid * up_part).astype(BF16)
    feed = scatter_sum(dot_rows(activated, down_w).astype(BF16), GROUP).astype(F32)
    feed_factor = norm_factor(feed)
    output = (residual + feed * feed_factor * gains[3]).astype(BF16)
    upstream = cotangent[0].astype(F32)
    feed_grad, gain_feed = norm_back(feed, feed_factor, gains[3], upstream)
    feed_grad_all = gather(feed_grad.astype(BF16), GROUP)
    act_grad = dot(feed_grad_all, down_w)
    gate_grad = act_grad * up_part * sigmoid * (1.0 + gate * (1.0 - sigmoid))
    up_grad = act_grad * (gate * sigmoid)
    gate_up_grad = jnp.concatenate([gate_grad.astype(BF16), up_grad.astype(BF16)], 1)
    back_feed = scatter_sum(dot_rows(gate_up_grad, gate_up_w).astype(BF16), GROUP).astype(F32)
    residual_grad = upstream + back_feed
    grad_gate_up = scatter_sum(dot_first(residual_all, gate_up_grad).astype(BF16), "chip")
    grad_gate_up = lax.all_to_all(grad_gate_up, "core", 0, 1, tiled=True)
    grad_gate_up = grad_gate_up.reshape(-1, cores, 2, hidden).astype(F32)
    grad_gate = grad_gate_up[:, :, 0].reshape(-1, cores * hidden)
    grad_up = grad_gate_up[:, :, 1].reshape(-1, cores * hidden)
    grad_down = scatter_sum(dot_first(feed_grad_all, activated).astype(BF16), "chip")
    grad_down = lax.all_to_all(grad_down, "core", 0, 1, tiled=True).astype(F32)
    projected_grad, gain_attn = norm_back(projected, proj_factor, gains[2], residual_grad)
    projected_all = gather(projected_grad.astype(BF16), GROUP)
    attended_grad = dot_rows(projected_all, out_w).astype(BF16).reshape(shape)
    share_grad = jnp.einsum("bqhd,bkhd->bhqk", attended_grad, value_low, preferred_element_type=F32)
    inner = jnp.sum(shares * share_grad, axis=-1, keepdims=True)
    score_grad = (shares * (share_grad - inner)).astype(BF16)
    query_grad = jnp.einsum("bhqk,bkhd->bqhd", score_grad, key_low, preferred_element_type=F32)
    key_grad = jnp.einsum("bhqk,bqhd->bkhd", score_grad, query_low, preferred_element_type=F32)
    value_grad = jnp.einsum(
        "bhqk,bqhd->bkhd", shares_low, attended_grad, preferred_element_type=F32
    )
    query_turn = rotate_back(query_grad * scale, cosine, sine).reshape(total_rows, part)
    key_turn = rotate_back(key_grad * scale, cosine, sine).reshape(total_rows, part)
    query_norm, key_norm = (query_raw * query_factor, key_raw * key_factor)
    sums = jnp.stack(
        [jnp.sum(gain_q * query_turn * query_norm, 1), jnp.sum(gain_k * key_turn * key_norm, 1)]
    )
    means = lax.psum(sums, GROUP) / width
    query_mixed = query_factor * (gain_q * query_turn - query_norm * means[0][:, None])
    key_mixed = key_factor * (gain_k * key_turn - key_norm * means[1][:, None])
    gain_query = jnp.sum(query_turn * query_norm, 0)
    gain_key = jnp.sum(key_turn * key_norm, 0)
    mixed_grad = jnp.concatenate(
        [query_mixed, key_mixed, value_grad.reshape(total_rows, part)], 1
    ).astype(BF16)
    input_part = dot_rows(mixed_grad, qkv_w).astype(BF16)
    input_grad = residual_grad + scatter_sum(input_part, GROUP).astype(F32)
    grad_qkv = scatter_sum(dot_first(tokens_all, mixed_grad).astype(BF16), "chip")
    grad_qkv = grad_qkv.reshape(members, qkv_rows, 3 * part)
    grad_qkv = lax.all_to_all(grad_qkv, GROUP, 0, 0, tiled=True)
    grad_qkv = grad_qkv.reshape(members, qkv_rows, 3, part).transpose(1, 2, 0, 3)
    grad_qkv = grad_qkv.reshape(qkv_rows, 3 * width).astype(F32)
    out_part = dot_first(attended_low, projected_all).astype(BF16)
    out_part = lax.dynamic_update_slice_in_dim(
        jnp.zeros((width, width), BF16), out_part, member * part, 0
    )
    grad_out = scatter_sum(out_part, ALL).astype(F32)
    wide = jnp.zeros((2, width), F32)
    wide = lax.dynamic_update_slice(wide, jnp.stack([gain_query, gain_key]), (0, member * part))
    grad_gains = lax.psum(jnp.concatenate([wide, gain_attn[None], gain_feed[None]]), ALL)
    return (
        output[None],
        input_grad[None],
        grad_qkv,
        grad_out,
        grad_gate,
        grad_up,
        grad_down,
        grad_gains,
    )


def solution(mesh):
    cores = 2
    chips = mesh.shape["dp"] // cores
    split = Mesh(mesh.devices.reshape(chips, cores, mesh.shape["ctx"]), ALL)
    dp = ("chip", "core")
    every = P((*dp, "ctx"), None)
    in_specs = (
        P(dp, "ctx", None),
        P(dp, "ctx"),
        every,
        every,
        P(dp, "ctx"),
        P(dp, "ctx"),
        P(dp, "ctx"),
        P(),
        P(dp, "ctx", None),
    )
    out_specs = (
        P(dp, "ctx", None),
        P(dp, "ctx", None),
        every,
        every,
        P(dp, "ctx"),
        P(dp, "ctx"),
        P(dp, "ctx"),
        P(),
    )
    return jax.shard_map(
        per_device, mesh=split, in_specs=in_specs, out_specs=out_specs, check_vma=False
    )
```

profile of v0, /device:TPU:0, one launch (start us, length us, event | category | flops | bytes accessed | tf_op | source)
XLA Modules:
  0.0 1303.3 jit_solution(13197521999439722919)
XLA Ops:
  9.9 26.9 %all_to_all.74 = bf16[8,64,768]{2,1,0:T(8,128)(2,1)} all-to-all(bf16[8,64,768]{2,1,0:T(8,128)(2,1)S(1)} %reshape.177), channel_id=1, replica_groups=mesh['chip'=4,'core'=2,'ctx'=4] {'core','ctx'}, dimensions={0} | all-to-all | bytes 1572864 | tf_op jit(solution)/shard_map/all_to_all | solution.py:83
  38.3 12.7 all-gather.1
  55.5 23.9 %all-gather.11.cloned.1.call-done = bf16[2048,768]{1,0:T(8,128)(2,1)} async-done(((bf16[512,768]{1,0:T(8,128)(2,1)}), bf16[2048,768]{1,0:T(8,128)(2,1)}) %all-gather.11.cloned.1.call-update) | async-done | bytes 3145744 | tf_op jit(solution)/shard_map/all_gather | solution.py:51
  79.3 48.8 %all-gather.25.cloned.1.call-done = bf16[1,1024,2048]{2,1,0:T(8,128)(2,1)} async-done(((bf16[1,128,2048]{2,1,0:T(8,128)(2,1)}), bf16[1,1024,2048]{2,1,0:T(8,128)(2,1)}) %all-gather.25.cloned.1.call-update) | async-done | bytes 4194320 | tf_op jit(solution)/shard_map/all_gather | solution.py:51
  128.1 6.2 fusion.3
  135.4 15.6 %psum.21 = f32[2,1024]{1,0:T(2,128)S(1)} all-reduce(f32[2,1024]{1,0:T(2,128)S(1)} %pad_maximum_fusion.10), channel_id=1, replica_groups=mesh['chip'=4,'core'=2,'ctx'=4] {'core','ctx'}, use_global_device_ids=true, to_apply=%region_2.0 | all-reduce | flops 2048 | bytes 16384 | tf_op jit(solution)/shard_map/psum | solution.py:100
  184.5 23.1 %all-gather.13.cloned.1.call-done = bf16[2048,2048]{1,0:T(8,128)(2,1)} async-done(((bf16[64,2048]{1,0:T(8,128)(2,1)}), bf16[2048,2048]{1,0:T(8,128)(2,1)}) %all-gather.13.cloned.1.call-update) | async-done | bytes 8388624 | tf_op jit(solution)/shard_map/all_gather | solution.py:51
  218.6 6.3 all_to_all.75
  228.9 71.0 %reduce-scatter.9.cloned.1.call-done = bf16[128,2048]{1,0:T(8,128)(2,1)} async-done(((bf16[1024,2048]{1,0:T(8,128)(2,1)}), bf16[128,2048]{1,0:T(8,128)(2,1)}) %reduce-scatter.9.cloned.1.call-update) | async-done | bytes 524304 | tf_op jit(solution)/shard_map/reduce_scatter | solution.py:55
  305.7 6.7 all_to_all.76
  315.1 74.5 %all-gather.17.cloned.1.call-done = bf16[2048,2048]{1,0:T(8,128)(2,1)} async-done(((bf16[512,2048]{1,0:T(8,128)(2,1)}), bf16[2048,2048]{1,0:T(8,128)(2,1)}) %all-gather.17.cloned.1.call-update) | async-done | bytes 8388624 | tf_op jit(solution)/shard_map/all_gather | solution.py:51
  389.6 49.2 %all-gather.15.cloned.1.call-done = bf16[1024,2048]{1,0:T(8,128)(2,1)} async-done(((bf16[128,2048]{1,0:T(8,128)(2,1)}), bf16[1024,2048]{1,0:T(8,128)(2,1)}) %all-gather.15.cloned.1.call-update) | async-done | bytes 4194320 | tf_op jit(solution)/shard_map/all_gather | solution.py:51
  438.8 12.5 fusion.74
  457.2 35.4 %all-gather.19.cloned.1.call-done = bf16[2048,1024]{1,0:T(8,128)(2,1)} async-done(((bf16[512,1024]{1,0:T(8,128)(2,1)}), bf16[2048,1024]{1,0:T(8,128)(2,1)}) %all-gather.19.cloned.1.call-update) | async-done | bytes 4194320 | tf_op jit(solution)/shard_map/all_gather | solution.py:51
  492.7 9.3 convolution_convert_fusion.5
  502.0 89.1 %reduce-scatter.11.cloned.1.call-done = bf16[128,2048]{1,0:T(8,128)(2,1)} async-done(((bf16[1024,2048]{1,0:T(8,128)(2,1)}), bf16[128,2048]{1,0:T(8,128)(2,1)}) %reduce-scatter.11.cloned.1.call-update) | async-done | bytes 524304 | tf_op jit(solution)/shard_map/reduce_scatter | solution.py:55
  596.6 46.8 %all-gather.21.cloned.1.call-done = bf16[1024,2048]{1,0:T(8,128)(2,1)} async-done(((bf16[128,2048]{1,0:T(8,128)(2,1)}), bf16[1024,2048]{1,0:T(8,128)(2,1)}) %all-gather.21.cloned.1.call-update) | async-done | bytes 4194320 | tf_op jit(solution)/shard_map/all_gather | solution.py:51
  643.4 11.6 multiply_convert_fusion.2
  657.1 12.7 convolution_convert_fusion.1
  669.8 87.8 %reduce-scatter.13.cloned.1.call-done = bf16[128,2048]{1,0:T(8,128)(2,1)} async-done(((bf16[1024,2048]{1,0:T(8,128)(2,1)}), bf16[128,2048]{1,0:T(8,128)(2,1)}) %reduce-scatter.13.cloned.1.call-update) | async-done | bytes 524304 | tf_op jit(solution)/shard_map/reduce_scatter | solution.py:55
  763.2 9.4 convolution_convert_fusion.4
  772.6 14.0 %convolution_convert_fusion = bf16[2048,2048]{1,0:T(8,128)(2,1)} fusion(bf16[1024,2048]{1,0:T(8,128)(2,1)} %all-gather.15.cloned.1.call-done, bf16[1024,1024]{1,0:T(8,128)(2,1)} %copy-done.24, bf16[1024,1024]{1,0:T(8,128)(2,1)} %copy-done.23), kind=kOutput, calls=%fused_computation.1 | convolution fusion | flops 8602517504 | bytes 16777216 | tf_op jit(solution)/shard_map/dot_general | solution.py:47
  786.9 22.9 %all-gather.23.cloned.1.call-done = bf16[1024,2048]{1,0:T(8,128)(2,1)} async-done(((bf16[128,2048]{1,0:T(8,128)(2,1)}), bf16[1024,2048]{1,0:T(8,128)(2,1)}) %all-gather.23.cloned.1.call-update) | async-done | bytes 4194320 | tf_op jit(solution)/shard_map/all_gather | solution.py:51
  830.7 15.6 %psum.22 = f32[2,1024]{1,0:T(2,128)S(1)} all-reduce(f32[2,1024]{1,0:T(2,128)S(1)} %pad_maximum_fusion.11), channel_id=1, replica_groups=mesh['chip'=4,'core'=2,'ctx'=4] {'core','ctx'}, use_global_device_ids=true, to_apply=%region_15.16 | all-reduce | flops 2048 | bytes 16384 | tf_op jit(solution)/shard_map/psum | solution.py:174
  849.5 6.2 fusion.10
  855.9 7.7 convolution_convert_fusion.3
  877.9 76.0 %reduce-scatter.21.cloned.1.call-done = bf16[512,2048]{1,0:T(8,128)(2,1)} async-done(((bf16[2048,2048]{1,0:T(8,128)(2,1)}), bf16[512,2048]{1,0:T(8,128)(2,1)}) %reduce-scatter.21.cloned.1.call-update) | async-done | bytes 2097168 | tf_op jit(solution)/shard_map/reduce_scatter | solution.py:55
  957.6 43.1 %reduce-scatter.17.cloned.1.call-done = bf16[512,768]{0,1:T(8,128)(2,1)} async-done(((bf16[2048,768]{0,1:T(8,128)(2,1)}), bf16[512,768]{0,1:T(8,128)(2,1)}) %reduce-scatter.17.cloned.1.call-update) | async-done | bytes 786448 | tf_op jit(solution)/shard_map/reduce_scatter | solution.py:55
  1007.6 64.0 %psum.23 = f32[4,2048]{1,0:T(4,128)} all-reduce(f32[4,2048]{1,0:T(4,128)S(1)} %pad_maximum_fusion.9), channel_id=1, replica_groups=mesh['chip'=4,'core'=2,'ctx'=4] {'chip','core','ctx'}, use_global_device_ids=true, to_apply=%region_25.26 | all-reduce | flops 8192 | bytes 65536 | tf_op jit(solution)/shard_map/psum | solution.py:196
  1074.1 6.6 reshape.191
  1080.7 7.3 fusion.67
  1108.9 185.7 %reduce-scatter.19.cloned.1.call-done = bf16[64,2048]{1,0:T(8,128)(2,1)} async-done(((bf16[2048,2048]{1,0:T(8,128)(2,1)}), bf16[64,2048]{1,0:T(8,128)(2,1)}) %reduce-scatter.19.cloned.1.call-update) | async-done | bytes 262160 | tf_op jit(solution)/shard_map/reduce_scatter | solution.py:55
  (181 shorter events, 160.0 us)
Async XLA Ops:
  7.2 72.2 %all-gather.11.cloned.1.call-start = ((), (), s32[]{:S(2)}) async-start(), calls=%async_computation.14 | async-start | bytes 3932160 | tf_op jit(solution)/shard_map/all_gather | solution.py:51
  7.2 31.1 %copy-start.21 = (s32[1,128]{1,0:T(1,128)S(1)}, s32[1,128]{1,0:T(1,128)}, u32[]{:S(2)}) copy-start(s32[1,128]{1,0:T(1,128)} %param.10) | copy-start | bytes 1540
  7.2 45.0 %copy-start.20 = (f32[4,2048]{1,0:T(4,128)S(1)}, f32[4,2048]{1,0:T(4,128)}, u32[]{:S(2)}) copy-start(f32[4,2048]{1,0:T(4,128)} %param.16) | copy-start | bytes 98308
  36.8 91.3 %all-gather.25.cloned.1.call-start = ((), (), s32[]{:S(2)}) async-start(), calls=%async_computation.29 | async-start | bytes 4718592 | tf_op jit(solution)/shard_map/all_gather | solution.py:51
  37.5 170.0 %all-gather.13.cloned.1.call-start = ((), (), s32[]{:S(2)}) async-start(), calls=%async_computation.15 | async-start | bytes 8650752 | tf_op jit(solution)/shard_map/all_gather | solution.py:51
  38.3 261.6 %reduce-scatter.9.cloned.1.call-start = ((), (), s32[]{:S(2)}) async-start(), calls=%async_computation.16 | async-start | bytes 4718592 | tf_op jit(solution)/shard_map/reduce_scatter | solution.py:55
  168.0 2.8 copy-start.13
  168.0 2.8 copy-start.14
  212.2 177.4 %all-gather.17.cloned.1.call-start = ((), (), s32[]{:S(2)}) async-start(), calls=%async_computation.18 | async-start | bytes 10485760 | tf_op jit(solution)/shard_map/all_gather | solution.py:51
  228.8 210.0 %all-gather.15.cloned.1.call-start = ((), (), s32[]{:S(2)}) async-start(), calls=%async_computation.17 | async-start | bytes 4718592 | tf_op jit(solution)/shard_map/all_gather | solution.py:51
  303.4 189.2 %all-gather.19.cloned.1.call-start = ((), (), s32[]{:S(2)}) async-start(), calls=%async_computation.19 | async-start | bytes 5242880 | tf_op jit(solution)/shard_map/all_gather | solution.py:51
  314.8 276.3 %reduce-scatter.11.cloned.1.call-start = ((), (), s32[]{:S(2)}) async-start(), calls=%async_computation.20 | async-start | bytes 4718592 | tf_op jit(solution)/shard_map/reduce_scatter | solution.py:55
  451.3 3.2 copy-start.7
  502.0 141.5 %all-gather.21.cloned.1.call-start = ((), (), s32[]{:S(2)}) async-start(), calls=%async_computation.21 | async-start | bytes 4718592 | tf_op jit(solution)/shard_map/all_gather | solution.py:51
  596.4 161.2 %reduce-scatter.13.cloned.1.call-start = ((), (), s32[]{:S(2)}) async-start(), calls=%async_computation.22 | async-start | bytes 4718592 | tf_op jit(solution)/shard_map/reduce_scatter | solution.py:55
  669.7 140.0 %all-gather.23.cloned.1.call-start = ((), (), s32[]{:S(2)}) async-start(), calls=%async_computation.23 | async-start | bytes 4718592 | tf_op jit(solution)/shard_map/all_gather | solution.py:51
  762.7 107.6 %reduce-scatter.23.cloned.1.call-start = ((), (), s32[]{:S(2)}) async-start(), calls=%async_computation.28 | async-start | bytes 5242880 | tf_op jit(solution)/shard_map/reduce_scatter | solution.py:55
  772.6 181.3 %reduce-scatter.21.cloned.1.call-start = ((), (), s32[]{:S(2)}) async-start(), calls=%async_computation.27 | async-start | bytes 10485760 | tf_op jit(solution)/shard_map/reduce_scatter | solution.py:55
  786.7 214.1 %reduce-scatter.17.cloned.1.call-start = ((), (), s32[]{:S(2)}) async-start(), calls=%async_computation.25 | async-start | bytes 3932160 | tf_op jit(solution)/shard_map/reduce_scatter | solution.py:55
  818.3 3.8 copy-start.9
  826.7 3.3 copy-start.2
  846.3 3.2 copy-start.18
  846.3 3.1 copy-start.22
  849.5 6.5 copy-start.19
  855.7 251.0 %reduce-scatter.15.cloned.1.call-start = ((), (), s32[]{:S(2)}) async-start(), calls=%async_computation.24 | async-start | bytes 4718592 | tf_op jit(solution)/shard_map/reduce_scatter | solution.py:55
  863.7 4.4 copy-start.6
  863.7 430.9 %reduce-scatter.19.cloned.1.call-start = ((), (), s32[]{:S(2)}) async-start(), calls=%async_computation.26 | async-start | bytes 8650752 | tf_op jit(solution)/shard_map/reduce_scatter | solution.py:55
  863.7 4.3 copy-start.1
  953.9 49.1 %all-to-all-start.4 = ((bf16[2,256,2048]{2,1,0:T(8,128)(2,1)}), bf16[2,256,2048]{2,1,0:T(8,128)(2,1)S(1)}, u32[]{:S(2)}, u32[]{:S(2)}) async-start(bf16[2,256,2048]{2,1,0:T(8,128)(2,1)} %bitcast.167), calls=%async_computation.11 | async-start | bytes 4194304 | tf_op jit(solution)/shard_map/all_to_all | solution.py:151
  1003.0 92.6 %all-to-all-start.3 = ((bf16[8,64,768]{2,1,0:T(8,128)(2,1)}), bf16[8,64,768]{2,1,0:T(8,128)(2,1)}, u32[]{:S(2)}, u32[]{:S(2)}) async-start(bf16[8,64,768]{2,1,0:T(8,128)(2,1)} %bitcast.33), calls=%async_computation.8 | async-start | bytes 1572864 | tf_op jit(solution)/shard_map/all_to_all | solution.py:186
  1095.6 11.0 copy-start
  1095.6 11.0 copy-start.8
  (11 other events, 19.2 us)
Sparse Core Ops, SparseCore 0:
  36.9 42.3 all-gather.10
  80.9 47.1 all-gather.24
  131.0 76.4 all-gather.12
  212.3 87.5 reduce-scatter.8
  302.2 87.3 all-gather.16
  391.6 47.1 all-gather.14
  441.2 51.4 all-gather.18
  502.1 88.9 reduce-scatter.10
  596.5 46.9 all-gather.20
  669.9 87.6 reduce-scatter.12
  762.9 46.8 all-gather.22
  812.6 51.4 reduce-scatter.22
  867.4 86.4 reduce-scatter.20
  956.7 43.9 reduce-scatter.16
  1002.9 103.7 reduce-scatter.14
  1108.8 185.7 reduce-scatter.18
where the time goes:
time: 1310 us; the launch traced here: 1300 us
  waiting for transfers between devices  885 us (68%)
  blocking collectives  153 us (12%)
  matrix products  116 us (9%)
  local copies, waits for them, and re-layouts  83.7 us (6%)
  other arithmetic  39.8 us (3%)
  between operations  14.9 us (1%)
    reduce_scatter x8, waiting for transfers between devices, scatter_sum(): return lax.psum_scatter(values, axes, scatter_dimension=0, tiled=True)  559 us
    all_gather x8, waiting for transfers between devices, gather(): return lax.all_gather(values, axes, axis=0, tiled=True)  325 us
    psum x1, blocking collectives, per_device(): lax.psum(jnp.concatenate([wide, gain_attn[None], gain_feed[None]]), ALL)  64 us
    dot_general x4, matrix products, dot(): return jnp.dot(left, right, preferred_element_type=F32)  34.9 us
    dot_general x4, matrix products, dot_rows(): lax.dot_general(left, right, (((1,), (1,)), ((), ())), preferred_element_...  34.2 us
    dot_general x4, matrix products, dot_first(): lax.dot_general(left, right, (((0,), (0,)), ((), ())), preferred_element_...  31.8 us
    all_to_all x1, blocking collectives, per_device(): qkv_cut = lax.all_to_all(qkv_cut, GROUP, 0, 0, tiled=True)  26.9 us
  transfers between devices with their start and end apart: 18, of which 15 were waited for; matrix products, arithmetic and copies ran while one was open for 14% of the time, Pallas kernels for 0%

commit v1 on v0

--- a/solution.py
+++ b/solution.py
@@ -193,7 +193,9 @@
     grad_out = scatter_sum(out_part, ALL).astype(F32)
     wide = jnp.zeros((2, width), F32)
     wide = lax.dynamic_update_slice(wide, jnp.stack([gain_query, gain_key]), (0, member * part))
-    grad_gains = lax.psum(jnp.concatenate([wide, gain_attn[None], gain_feed[None]]), ALL)
+    grad_gains = lax.psum(
+        lax.psum(jnp.concatenate([wide, gain_attn[None], gain_feed[None]]), "chip"), ("core", "ctx")
+    )
     return (
         output[None],
         input_grad[None],

time: 1310 us -> 1320 us (level)
  waiting for transfers between devices: 885 us -> 934 us
  blocking collectives: 153 us -> 120 us
    psum x1, blocking collectives: 64 us -> 16.8 us  [per_device(): lax.psum(jnp.concatenate([wide, gain_attn[None], gain_feed[None]]), 'chip')]
    reduce_scatter x8, waiting for transfers between devices: 559 us -> 578 us  [scatter_sum(): return lax.psum_scatter(values, axes, scatter_dimension=0, tiled=True)]
    all_to_all x1, waiting for transfers between devices: 0.01 us -> 15.9 us  [per_device(): grad_qkv = lax.all_to_all(grad_qkv, GROUP, 0, 0, tiled=True)]
    all_gather x8, waiting for transfers between devices: 325 us -> 339 us  [gather(): return lax.all_gather(values, axes, axis=0, tiled=True)]
    unnamed x62 -> x68, local copies, waits for them, and re-layouts: 25.5 us -> 26.9 us
  transfers between devices with their start and end apart: 18 -> 18, of which waited for: 15 -> 16; matrix products, arithmetic and copies ran while one was open for 14% -> 14% of each run, Pallas kernels for 0% -> 0%
where the time goes in v1:
time: 1320 us
  waiting for transfers between devices  934 us (71%)
  blocking collectives  120 us (9%)
  matrix products  116 us (9%)
  local copies, waits for them, and re-layouts  84.9 us (6%)
  other arithmetic  39.8 us (3%)
  between operations  14.8 us (1%)
    reduce_scatter x8, waiting for transfers between devices, scatter_sum(): return lax.psum_scatter(values, axes, scatter_dimension=0, tiled=True)  578 us
    all_gather x8, waiting for transfers between devices, gather(): return lax.all_gather(values, axes, axis=0, tiled=True)  339 us
    dot_general x4, matrix products, dot(): return jnp.dot(left, right, preferred_element_type=F32)  34.9 us
    dot_general x4, matrix products, dot_rows(): lax.dot_general(left, right, (((1,), (1,)), ((), ())), preferred_element_...  33.7 us
    dot_general x4, matrix products, dot_first(): lax.dot_general(left, right, (((0,), (0,)), ((), ())), preferred_element_...  31.6 us
    psum x1, blocking collectives, per_device(): means = lax.psum(sums, GROUP) / width  28 us
    unnamed x68, local copies, waits for them, and re-layouts  26.9 us
    all_to_all x1, blocking collectives, per_device(): qkv_cut = lax.all_to_all(qkv_cut, GROUP, 0, 0, tiled=True)  26.9 us
  transfers between devices with their start and end apart: 18, of which 16 were waited for; matrix products, arithmetic and copies ran while one was open for 14% of the time, Pallas kernels for 0%

profile of v1, /device:TPU:0, one launch (start us, length us, event | category | flops | bytes accessed | tf_op | source)
XLA Modules:
  0.0 1318.8 jit_solution(9574531186830737172)
XLA Ops:
  9.9 26.9 %all_to_all.74 = bf16[8,64,768]{2,1,0:T(8,128)(2,1)} all-to-all(bf16[8,64,768]{2,1,0:T(8,128)(2,1)S(1)} %reshape.177), channel_id=1, replica_groups=mesh['chip'=4,'core'=2,'ctx'=4] {'core','ctx'}, dimensions={0} | all-to-all | bytes 1572864 | tf_op jit(solution)/shard_map/all_to_all | solution.py:83
  38.3 12.7 all-gather.1
  55.4 23.9 %all-gather.11.cloned.1.call-done = bf16[2048,768]{1,0:T(8,128)(2,1)} async-done(((bf16[512,768]{1,0:T(8,128)(2,1)}), bf16[2048,768]{1,0:T(8,128)(2,1)}) %all-gather.11.cloned.1.call-update) | async-done | bytes 3145744 | tf_op jit(solution)/shard_map/all_gather | solution.py:51
  79.3 48.8 %all-gather.25.cloned.1.call-done = bf16[1,1024,2048]{2,1,0:T(8,128)(2,1)} async-done(((bf16[1,128,2048]{2,1,0:T(8,128)(2,1)}), bf16[1,1024,2048]{2,1,0:T(8,128)(2,1)}) %all-gather.25.cloned.1.call-update) | async-done | bytes 4194320 | tf_op jit(solution)/shard_map/all_gather | solution.py:51
  135.4 15.6 %psum.28 = f32[2,1024]{1,0:T(2,128)S(1)} all-reduce(f32[2,1024]{1,0:T(2,128)S(1)} %pad_maximum_fusion.10), channel_id=1, replica_groups=mesh['chip'=4,'core'=2,'ctx'=4] {'core','ctx'}, use_global_device_ids=true, to_apply=%region_2.0 | all-reduce | flops 2048 | bytes 16384 | tf_op jit(solution)/shard_map/psum | solution.py:100
  184.5 23.1 %all-gather.13.cloned.1.call-done = bf16[2048,2048]{1,0:T(8,128)(2,1)} async-done(((bf16[64,2048]{1,0:T(8,128)(2,1)}), bf16[2048,2048]{1,0:T(8,128)(2,1)}) %all-gather.13.cloned.1.call-update) | async-done | bytes 8388624 | tf_op jit(solution)/shard_map/all_gather | solution.py:51
  228.9 71.0 %reduce-scatter.9.cloned.1.call-done = bf16[128,2048]{1,0:T(8,128)(2,1)} async-done(((bf16[1024,2048]{1,0:T(8,128)(2,1)}), bf16[128,2048]{1,0:T(8,128)(2,1)}) %reduce-scatter.9.cloned.1.call-update) | async-done | bytes 524304 | tf_op jit(solution)/shard_map/reduce_scatter | solution.py:55
  305.8 6.6 all_to_all.76
  315.1 74.5 %all-gather.17.cloned.1.call-done = bf16[2048,2048]{1,0:T(8,128)(2,1)} async-done(((bf16[512,2048]{1,0:T(8,128)(2,1)}), bf16[2048,2048]{1,0:T(8,128)(2,1)}) %all-gather.17.cloned.1.call-update) | async-done | bytes 8388624 | tf_op jit(solution)/shard_map/all_gather | solution.py:51
  389.6 49.2 %all-gather.15.cloned.1.call-done = bf16[1024,2048]{1,0:T(8,128)(2,1)} async-done(((bf16[128,2048]{1,0:T(8,128)(2,1)}), bf16[1024,2048]{1,0:T(8,128)(2,1)}) %all-gather.15.cloned.1.call-update) | async-done | bytes 4194320 | tf_op jit(solution)/shard_map/all_gather | solution.py:51
  438.8 12.5 fusion.74
  457.3 35.4 %all-gather.19.cloned.1.call-done = bf16[2048,1024]{1,0:T(8,128)(2,1)} async-done(((bf16[512,1024]{1,0:T(8,128)(2,1)}), bf16[2048,1024]{1,0:T(8,128)(2,1)}) %all-gather.19.cloned.1.call-update) | async-done | bytes 4194320 | tf_op jit(solution)/shard_map/all_gather | solution.py:51
  492.7 9.3 convolution_convert_fusion.5
  502.0 89.1 %reduce-scatter.11.cloned.1.call-done = bf16[128,2048]{1,0:T(8,128)(2,1)} async-done(((bf16[1024,2048]{1,0:T(8,128)(2,1)}), bf16[128,2048]{1,0:T(8,128)(2,1)}) %reduce-scatter.11.cloned.1.call-update) | async-done | bytes 524304 | tf_op jit(solution)/shard_map/reduce_scatter | solution.py:55
  596.7 46.8 %all-gather.21.cloned.1.call-done = bf16[1024,2048]{1,0:T(8,128)(2,1)} async-done(((bf16[128,2048]{1,0:T(8,128)(2,1)}), bf16[1024,2048]{1,0:T(8,128)(2,1)}) %all-gather.21.cloned.1.call-update) | async-done | bytes 4194320 | tf_op jit(solution)/shard_map/all_gather | solution.py:51
  643.5 11.6 multiply_convert_fusion.2
  657.1 12.6 convolution_convert_fusion.1
  669.8 87.8 %reduce-scatter.13.cloned.1.call-done = bf16[128,2048]{1,0:T(8,128)(2,1)} async-done(((bf16[1024,2048]{1,0:T(8,128)(2,1)}), bf16[128,2048]{1,0:T(8,128)(2,1)}) %reduce-scatter.13.cloned.1.call-update) | async-done | bytes 524304 | tf_op jit(solution)/shard_map/reduce_scatter | solution.py:55
  762.8 9.4 convolution_convert_fusion.4
  772.6 37.1 %all-gather.23.cloned.1.call-done = bf16[1024,2048]{1,0:T(8,128)(2,1)} async-done(((bf16[128,2048]{1,0:T(8,128)(2,1)}), bf16[1024,2048]{1,0:T(8,128)(2,1)}) %all-gather.23.cloned.1.call-update) | async-done | bytes 4194320 | tf_op jit(solution)/shard_map/all_gather | solution.py:51
  830.7 16.8 %psum.30 = f32[4,2048]{1,0:T(4,128)S(1)} all-reduce(f32[4,2048]{1,0:T(4,128)S(1)} %pad_maximum_fusion.9), channel_id=1, replica_groups=mesh['chip'=4,'core'=2,'ctx'=4] {'chip'}, use_global_device_ids=true, to_apply=%region_25.26 | all-reduce | flops 8192 | bytes 65536 | tf_op jit(solution)/shard_map/psum | solution.py:197
  847.5 28.0 %all-reduce = (f32[2,1024]{1,0:T(2,128)S(1)}, f32[4,2048]{1,0:T(4,128)}) all-reduce(f32[2,1024]{1,0:T(2,128)S(1)} %pad_maximum_fusion.11, f32[4,2048]{1,0:T(4,128)S(1)} %psum.30), channel_id=1, replica_groups=mesh['chip'=4,'core'=2,'ctx'=4] {'core','ctx'}, use_global_device_ids=true, to_apply=%region_15.16 | all-reduce | flops 10240 | bytes 81920 | tf_op jit(solution)/shard_map/psum | solution.py:174
  885.0 13.6 %convolution_convert_fusion = bf16[2048,2048]{1,0:T(8,128)(2,1)} fusion(bf16[1024,2048]{1,0:T(8,128)(2,1)} %all-gather.15.cloned.1.call-done, bf16[1024,1024]{1,0:T(8,128)(2,1)} %copy-done.27, bf16[1024,1024]{1,0:T(8,128)(2,1)S(1)} %copy-done.26), kind=kOutput, calls=%fused_computation.1 | convolution fusion | flops 8602517504 | bytes 16777216 | tf_op jit(solution)/shard_map/dot_general | solution.py:47
  900.1 7.2 convolution_convert_fusion.3
  917.7 9.2 reduce-scatter.17.cloned.1.call-done
  929.2 87.4 %reduce-scatter.21.cloned.1.call-done = bf16[512,2048]{1,0:T(8,128)(2,1)} async-done(((bf16[2048,2048]{1,0:T(8,128)(2,1)}), bf16[512,2048]{1,0:T(8,128)(2,1)}) %reduce-scatter.21.cloned.1.call-update) | async-done | bytes 2097168 | tf_op jit(solution)/shard_map/reduce_scatter | solution.py:55
  1016.5 6.6 all_to_all.77
  1032.2 6.6 reshape.191
  1038.8 7.2 fusion.67
  1053.6 15.9 %all-to-all-done.3 = bf16[8,64,768]{2,1,0:T(8,128)(2,1)} async-done(((bf16[8,64,768]{2,1,0:T(8,128)(2,1)}), bf16[8,64,768]{2,1,0:T(8,128)(2,1)}, u32[]{:S(2)}, u32[]{:S(2)}) %all-to-all-start.3) | async-done | bytes 786464 | tf_op jit(solution)/shard_map/all_to_all | solution.py:186
  1074.6 46.3 %reduce-scatter.15.cloned.1.call-done = bf16[128,2048]{1,0:T(8,128)(2,1)} async-done(((bf16[1024,2048]{1,0:T(8,128)(2,1)}), bf16[128,2048]{1,0:T(8,128)(2,1)}) %reduce-scatter.15.cloned.1.call-update) | async-done | bytes 524304 | tf_op jit(solution)/shard_map/reduce_scatter | solution.py:55
  1123.1 187.2 %reduce-scatter.19.cloned.1.call-done = bf16[64,2048]{1,0:T(8,128)(2,1)} async-done(((bf16[2048,2048]{1,0:T(8,128)(2,1)}), bf16[64,2048]{1,0:T(8,128)(2,1)}) %reduce-scatter.19.cloned.1.call-update) | async-done | bytes 262160 | tf_op jit(solution)/shard_map/reduce_scatter | solution.py:55
  (187 shorter events, 168.3 us)
Async XLA Ops:
  7.2 72.2 %all-gather.11.cloned.1.call-start = ((), (), s32[]{:S(2)}) async-start(), calls=%async_computation.14 | async-start | bytes 3932160 | tf_op jit(solution)/shard_map/all_gather | solution.py:51
  7.2 31.1 %copy-start.23 = (s32[1,128]{1,0:T(1,128)S(1)}, s32[1,128]{1,0:T(1,128)}, u32[]{:S(2)}) copy-start(s32[1,128]{1,0:T(1,128)} %param.10) | copy-start | bytes 1540
  7.2 45.0 %copy-start.22 = (f32[4,2048]{1,0:T(4,128)S(1)}, f32[4,2048]{1,0:T(4,128)}, u32[]{:S(2)}) copy-start(f32[4,2048]{1,0:T(4,128)} %param.16) | copy-start | bytes 98308
  36.8 91.3 %all-gather.25.cloned.1.call-start = ((), (), s32[]{:S(2)}) async-start(), calls=%async_computation.29 | async-start | bytes 4718592 | tf_op jit(solution)/shard_map/all_gather | solution.py:51
  37.5 170.0 %all-gather.13.cloned.1.call-start = ((), (), s32[]{:S(2)}) async-start(), calls=%async_computation.15 | async-start | bytes 8650752 | tf_op jit(solution)/shard_map/all_gather | solution.py:51
  38.3 261.7 %reduce-scatter.9.cloned.1.call-start = ((), (), s32[]{:S(2)}) async-start(), calls=%async_computation.16 | async-start | bytes 4718592 | tf_op jit(solution)/shard_map/reduce_scatter | solution.py:55
  168.0 2.8 copy-start.13
  168.0 2.8 copy-start.14
  212.2 177.4 %all-gather.17.cloned.1.call-start = ((), (), s32[]{:S(2)}) async-start(), calls=%async_computation.18 | async-start | bytes 10485760 | tf_op jit(solution)/shard_map/all_gather | solution.py:51
  228.9 209.9 %all-gather.15.cloned.1.call-start = ((), (), s32[]{:S(2)}) async-start(), calls=%async_computation.17 | async-start | bytes 4718592 | tf_op jit(solution)/shard_map/all_gather | solution.py:51
  303.4 189.2 %all-gather.19.cloned.1.call-start = ((), (), s32[]{:S(2)}) async-start(), calls=%async_computation.19 | async-start | bytes 5242880 | tf_op jit(solution)/shard_map/all_gather | solution.py:51
  314.9 276.3 %reduce-scatter.11.cloned.1.call-start = ((), (), s32[]{:S(2)}) async-start(), calls=%async_computation.20 | async-start | bytes 4718592 | tf_op jit(solution)/shard_map/reduce_scatter | solution.py:55
  451.3 3.3 copy-start.7
  502.0 141.5 %all-gather.21.cloned.1.call-start = ((), (), s32[]{:S(2)}) async-start(), calls=%async_computation.21 | async-start | bytes 4718592 | tf_op jit(solution)/shard_map/all_gather | solution.py:51
  596.4 161.2 %reduce-scatter.13.cloned.1.call-start = ((), (), s32[]{:S(2)}) async-start(), calls=%async_computation.22 | async-start | bytes 4718592 | tf_op jit(solution)/shard_map/reduce_scatter | solution.py:55
  669.7 140.0 %all-gather.23.cloned.1.call-start = ((), (), s32[]{:S(2)}) async-start(), calls=%async_computation.23 | async-start | bytes 4718592 | tf_op jit(solution)/shard_map/all_gather | solution.py:51
  762.7 151.4 %reduce-scatter.23.cloned.1.call-start = ((), (), s32[]{:S(2)}) async-start(), calls=%async_computation.28 | async-start | bytes 5242880 | tf_op jit(solution)/shard_map/reduce_scatter | solution.py:55
  772.2 154.7 %reduce-scatter.17.cloned.1.call-start = ((), (), s32[]{:S(2)}) async-start(), calls=%async_computation.25 | async-start | bytes 3932160 | tf_op jit(solution)/shard_map/reduce_scatter | solution.py:55
  818.3 3.8 copy-start.9
  826.7 3.3 copy-start.2
  875.5 3.1 copy-start.19
  875.5 3.1 copy-start.24
  878.7 6.3 copy-start.26
  884.9 131.6 %reduce-scatter.21.cloned.1.call-start = ((), (), s32[]{:S(2)}) async-start(), calls=%async_computation.27 | async-start | bytes 10485760 | tf_op jit(solution)/shard_map/reduce_scatter | solution.py:55
  898.6 222.2 %reduce-scatter.15.cloned.1.call-start = ((), (), s32[]{:S(2)}) async-start(), calls=%async_computation.24 | async-start | bytes 4718592 | tf_op jit(solution)/shard_map/reduce_scatter | solution.py:55
  907.3 4.4 copy-start.6
  907.3 403.0 %reduce-scatter.19.cloned.1.call-start = ((), (), s32[]{:S(2)}) async-start(), calls=%async_computation.26 | async-start | bytes 8650752 | tf_op jit(solution)/shard_map/reduce_scatter | solution.py:55
  907.4 4.3 copy-start.1
  914.1 15.0 %all-to-all-start.5 = ((bf16[2,256,1024]{2,1,0:T(8,128)(2,1)}), bf16[2,256,1024]{2,1,0:T(8,128)(2,1)S(1)}, u32[]{:S(2)}, u32[]{:S(2)}) async-start(bf16[2,256,1024]{2,1,0:T(8,128)(2,1)} %bitcast.174), calls=%async_computation.13 | async-start | bytes 2097152 | tf_op jit(solution)/shard_map/all_to_all | solution.py:156
  1023.1 46.4 %all-to-all-start.3 = ((bf16[8,64,768]{2,1,0:T(8,128)(2,1)}), bf16[8,64,768]{2,1,0:T(8,128)(2,1)}, u32[]{:S(2)}, u32[]{:S(2)}) async-start(bf16[8,64,768]{2,1,0:T(8,128)(2,1)} %bitcast.167), calls=%async_computation.8 | async-start | bytes 1572864 | tf_op jit(solution)/shard_map/all_to_all | solution.py:186
  1053.6 67.2 %copy-start = (bf16[1,128,2048]{2,1,0:T(8,128)(2,1)S(1)}, bf16[1,128,2048]{2,1,0:T(8,128)(2,1)}, u32[]{:S(2)}) copy-start(bf16[1,128,2048]{2,1,0:T(8,128)(2,1)} %param.17) | copy-start | bytes 1572868
  1053.6 67.2 %copy-start.8 = (bf16[128,2048]{1,0:T(8,128)(2,1)S(1)}, bf16[128,2048]{1,0:T(8,128)(2,1)}, u32[]{:S(2)}) copy-start(bf16[128,2048]{1,0:T(8,128)(2,1)} %reduce-scatter.13.cloned.1.call-done) | copy-start | bytes 1572868
  (14 other events, 23.1 us)
Sparse Core Ops, SparseCore 0:
  36.9 42.3 all-gather.10
  80.9 47.1 all-gather.24
  131.0 76.4 all-gather.12
  212.3 87.5 reduce-scatter.8
  302.2 87.3 all-gather.16
  391.6 47.1 all-gather.14
  441.2 51.4 all-gather.18
  502.1 88.9 reduce-scatter.10
  596.5 46.8 all-gather.20
  669.9 87.6 reduce-scatter.12
  762.9 46.8 all-gather.22
  812.6 52.2 reduce-scatter.22
  885.0 41.7 reduce-scatter.16
  930.1 86.3 reduce-scatter.20
  1018.6 102.1 reduce-scatter.14
  1123.0 187.2 reduce-scatter.18
